TPU v7x, 256 devices: a whole 4x4x8 slice. The times are simulated.
256 devices in a mesh: nodes: 128 (over y, z, x), params: 2 (over core).
Axes of the slice: x: 4, y: 4, z: 8, core: 2. Of those that a mesh axis runs over, the one named last changes fastest.
Arguments:
- snapshots: bfloat16 [128, 48, 131072], P('params', None, 'nodes'), may hold values from -6 to 6
- space_start: float32 [64, 131072], P(None, 'nodes'), may hold values from -12 to 12
- time_start: float32 [64, 48], replicated, may hold values from -0.9 to 0.9
Outputs:
- space_factor: float32 [64, 131072], P(None, 'nodes')
- param_factor: float32 [64, 128], P(None, 'params')
- time_factor: float32 [64, 48], replicated
All inputs are finite; a program needn't handle non-finite values.
Results may differ from a plain program's by a relative error of at most 0.0093.
Values sent between devices are 32-bit elements; how exact they have to be, the bound alone decides.
No kernel may reach another device: no remote copies, remote signals or barrier semaphores. Data moves between devices by JAX's collectives and lax.ppermute only.
A program may use at most 64 MiB of HBM per device.

v0:
```python
import jax
import jax.numpy as jnp
from jax import lax
from jax.sharding import Mesh
from jax.sharding import PartitionSpec as P

SWEEPS = 4
NODES = ("nodes_0", "nodes_1", "nodes_2")


ridge_share = 0.01


def copy_for_each(x, axis):
    copies = jnp.broadcast_to(x, (lax.axis_size(axis), *x.shape))
    return lax.all_to_all(copies, axis, split_axis=0, concat_axis=0, tiled=True)


def taken_together(x, axis):
    everything = copy_for_each(x, axis)
    return jnp.sum(everything, axis=0)


def one_axis_at_a_time(x, axes):
    far, near = axes
    nearer = taken_together(x, near)
    return taken_together(nearer, far)


def gram_of(factor):
    return jnp.dot(factor, factor.T, precision=lax.Precision.HIGHEST)


def solve_gram(gram, right_side):
    count = gram.shape[0]
    ridge_term = ridge_share * jnp.trace(gram) / count
    matrix = gram + ridge_term * jnp.eye(count, dtype=gram.dtype)
    chol_factor = jnp.linalg.cholesky(matrix)
    return jax.scipy.linalg.cho_solve((chol_factor, True), right_side)


def per_device(snapshots, space_start, time_start):
    param_rows, step_count, node_cols = snapshots.shape
    columns = space_start.shape[0]
    unfolded = snapshots.reshape(param_rows * step_count, node_cols)
    space_factor = space_start
    time_factor = time_start
    param_factor = None
    for sweep_index in range(SWEEPS):
        space_low = space_factor.astype(jnp.bfloat16)
        contracted = jnp.dot(unfolded, space_low.T, preferred_element_type=jnp.float32).reshape(
            param_rows, step_count, columns
        )
        space_part = gram_of(space_factor)
        time_gram = gram_of(time_factor)
        param_part = jnp.einsum(
            "jkr,rk->rj", contracted, time_factor, precision=lax.Precision.HIGHEST
        )
        param_side, space_gram = (
            one_axis_at_a_time(param_part, (("nodes_0", "nodes_1"), "nodes_2")),
            one_axis_at_a_time(space_part, (("nodes_0", "nodes_1"), "nodes_2")),
        )
        param_factor = solve_gram(space_gram * time_gram, param_side)
        param_gram = taken_together(gram_of(param_factor), "params")
        time_part = jnp.einsum(
            "jkr,rj->rk", contracted, param_factor, precision=lax.Precision.HIGHEST
        )
        time_side = one_axis_at_a_time(time_part, (("nodes_0", "nodes_1"), ("nodes_2", "params")))
        time_factor = solve_gram(space_gram * param_gram, time_side)
        khatri = (
            (param_factor[:, :, None] * time_factor[:, None, :])
            .astype(jnp.bfloat16)
            .reshape(columns, param_rows * step_count)
        )
        space_part_side = jnp.dot(khatri, unfolded, preferred_element_type=jnp.float32)
        system = param_gram * gram_of(time_factor)
        space_side = taken_together(space_part_side, "params")
        space_factor = solve_gram(system, space_side)
    return (space_factor, param_factor, time_factor)


def solution(mesh):
    split = Mesh(
        mesh.devices.reshape(4, 8, 4, mesh.shape["params"]),
        ("nodes_0", "nodes_1", "nodes_2", "params"),
    )
    return jax.shard_map(
        per_device,
        mesh=split,
        in_specs=(P("params", None, NODES), P(None, NODES), P()),
        out_specs=(P(None, NODES), P(None, "params"), P()),
        check_vma=False,
    )
```

profile of v0, /device:TPU:1, one launch (start us, length us, event | category | flops | bytes accessed | tf_op | source)
XLA Modules:
  0.0 589.2 jit_solution(1397251537108570877)
XLA Ops:
  21.9 11.2 %all-to-all-start.1 = ((f32[32,1,4096]{2,1,0:T(1,128)}), f32[32,1,4096]{2,1,0:T(1,128)S(1)}, u32[]{:S(2)}, u32[]{:S(2)}) async-start(f32[32,1,4096]{2,1,0:T(1,128)} %reshape.84), calls=%async_computation.1 | async-start | bytes 1048576 | tf_op jit(solution)/shard_map/all_to_all | solution.py:16
  35.7 9.8 %all-to-all-done.1 = f32[32,1,4096]{2,1,0:T(1,128)S(1)} async-done(((f32[32,1,4096]{2,1,0:T(1,128)}), f32[32,1,4096]{2,1,0:T(1,128)S(1)}, u32[]{:S(2)}, u32[]{:S(2)}) %all-to-all-start.1) | async-done | bytes 524320 | tf_op jit(solution)/shard_map/all_to_all | solution.py:16
  46.3 7.8 %all-to-all-start.3 = ((f32[32,1,4096]{2,1,0:T(1,128)}), f32[32,1,4096]{2,1,0:T(1,128)}, u32[]{:S(2)}, u32[]{:S(2)}) async-start(f32[32,1,4096]{2,1,0:T(1,128)} %reshape.80), calls=%async_computation.3 | async-start | bytes 1048576 | tf_op jit(solution)/shard_map/all_to_all | solution.py:16
  75.6 7.0 %all_to_all.160 = f32[2,1,4096]{2,1,0:T(1,128)S(1)} all-to-all(f32[2,1,4096]{2,1,0:T(1,128)S(1)} %reshape.90), channel_id=1, replica_groups=mesh['nodes_0'=4,'nodes_1'=8,'nodes_2'=4,'params'=2] {'params'}, dimensions={0} | all-to-all | bytes 65536 | tf_op jit(solution)/shard_map/all_to_all | solution.py:16
  95.5 9.4 %all-to-all-start.6 = ((f32[32,1,3072]{2,1,0:T(1,128)}), f32[32,1,3072]{2,1,0:T(1,128)S(1)}, u32[]{:S(2)}, u32[]{:S(2)}) async-start(f32[32,1,3072]{2,1,0:T(1,128)} %reshape.88), calls=%async_computation.6 | async-start | bytes 786432 | tf_op jit(solution)/shard_map/all_to_all | solution.py:16
  105.1 5.8 cholesky.205
  125.1 5.8 cholesky.216
  137.2 7.1 %all_to_all.161 = f32[2,64,1024]{2,1,0:T(8,128)S(1)} all-to-all(f32[2,64,1024]{2,1,0:T(8,128)S(1)} %broadcast_in_dim.128), channel_id=1, replica_groups=mesh['nodes_0'=4,'nodes_1'=8,'nodes_2'=4,'params'=2] {'params'}, dimensions={0} | all-to-all | bytes 1048576 | tf_op jit(solution)/shard_map/all_to_all | solution.py:16
  168.5 7.4 %all-to-all-start.9 = ((f32[32,1,4096]{2,1,0:T(1,128)}), f32[32,1,4096]{2,1,0:T(1,128)}, u32[]{:S(2)}, u32[]{:S(2)}) async-start(f32[32,1,4096]{2,1,0:T(1,128)} %reshape.98), calls=%async_computation.9 | async-start | bytes 1048576 | tf_op jit(solution)/shard_map/all_to_all | solution.py:16
  178.5 10.2 %all-to-all-done.9 = f32[32,1,4096]{2,1,0:T(1,128)} async-done(((f32[32,1,4096]{2,1,0:T(1,128)}), f32[32,1,4096]{2,1,0:T(1,128)}, u32[]{:S(2)}, u32[]{:S(2)}) %all-to-all-start.9) | async-done | bytes 524320 | tf_op jit(solution)/shard_map/all_to_all | solution.py:16
  188.7 8.0 %all-to-all-start.11 = ((f32[32,1,4096]{2,1,0:T(1,128)}), f32[32,1,4096]{2,1,0:T(1,128)}, u32[]{:S(2)}, u32[]{:S(2)}) async-start(f32[32,1,4096]{2,1,0:T(1,128)} %reshape.94), calls=%async_computation.11 | async-start | bytes 1048576 | tf_op jit(solution)/shard_map/all_to_all | solution.py:16
  203.5 5.8 cholesky.227
  223.6 6.3 %all_to_all.162 = f32[2,1,4096]{2,1,0:T(1,128)S(1)} all-to-all(f32[2,1,4096]{2,1,0:T(1,128)S(1)} %reshape.104), channel_id=1, replica_groups=mesh['nodes_0'=4,'nodes_1'=8,'nodes_2'=4,'params'=2] {'params'}, dimensions={0} | all-to-all | bytes 65536 | tf_op jit(solution)/shard_map/all_to_all | solution.py:16
  242.6 9.8 %all-to-all-start.14 = ((f32[32,1,3072]{2,1,0:T(1,128)}), f32[32,1,3072]{2,1,0:T(1,128)S(1)}, u32[]{:S(2)}, u32[]{:S(2)}) async-start(f32[32,1,3072]{2,1,0:T(1,128)} %reshape.102), calls=%async_computation.14 | async-start | bytes 786432 | tf_op jit(solution)/shard_map/all_to_all | solution.py:16
  252.6 5.8 cholesky.238
  268.5 5.8 cholesky.249
  284.7 7.0 %all_to_all.163 = f32[2,64,1024]{2,1,0:T(8,128)S(1)} all-to-all(f32[2,64,1024]{2,1,0:T(8,128)S(1)} %broadcast_in_dim.136), channel_id=1, replica_groups=mesh['nodes_0'=4,'nodes_1'=8,'nodes_2'=4,'params'=2] {'params'}, dimensions={0} | all-to-all | bytes 1048576 | tf_op jit(solution)/shard_map/all_to_all | solution.py:16
  315.8 7.7 %all-to-all-start.17 = ((f32[32,1,4096]{2,1,0:T(1,128)}), f32[32,1,4096]{2,1,0:T(1,128)}, u32[]{:S(2)}, u32[]{:S(2)}) async-start(f32[32,1,4096]{2,1,0:T(1,128)} %reshape.112), calls=%async_computation.17 | async-start | bytes 1048576 | tf_op jit(solution)/shard_map/all_to_all | solution.py:16
  326.0 10.3 %all-to-all-done.17 = f32[32,1,4096]{2,1,0:T(1,128)} async-done(((f32[32,1,4096]{2,1,0:T(1,128)}), f32[32,1,4096]{2,1,0:T(1,128)}, u32[]{:S(2)}, u32[]{:S(2)}) %all-to-all-start.17) | async-done | bytes 524320 | tf_op jit(solution)/shard_map/all_to_all | solution.py:16
  336.3 8.3 %all-to-all-start.19 = ((f32[32,1,4096]{2,1,0:T(1,128)}), f32[32,1,4096]{2,1,0:T(1,128)}, u32[]{:S(2)}, u32[]{:S(2)}) async-start(f32[32,1,4096]{2,1,0:T(1,128)} %reshape.108), calls=%async_computation.19 | async-start | bytes 1048576 | tf_op jit(solution)/shard_map/all_to_all | solution.py:16
  351.3 5.8 cholesky.260
  371.5 6.3 %all_to_all.164 = f32[2,1,4096]{2,1,0:T(1,128)S(1)} all-to-all(f32[2,1,4096]{2,1,0:T(1,128)S(1)} %reshape.118), channel_id=1, replica_groups=mesh['nodes_0'=4,'nodes_1'=8,'nodes_2'=4,'params'=2] {'params'}, dimensions={0} | all-to-all | bytes 65536 | tf_op jit(solution)/shard_map/all_to_all | solution.py:16
  390.4 9.8 %all-to-all-start.22 = ((f32[32,1,3072]{2,1,0:T(1,128)}), f32[32,1,3072]{2,1,0:T(1,128)S(1)}, u32[]{:S(2)}, u32[]{:S(2)}) async-start(f32[32,1,3072]{2,1,0:T(1,128)} %reshape.116), calls=%async_computation.22 | async-start | bytes 786432 | tf_op jit(solution)/shard_map/all_to_all | solution.py:16
  416.4 5.8 cholesky.282
  432.5 7.0 %all_to_all.165 = f32[2,64,1024]{2,1,0:T(8,128)S(1)} all-to-all(f32[2,64,1024]{2,1,0:T(8,128)S(1)} %broadcast_in_dim.144), channel_id=1, replica_groups=mesh['nodes_0'=4,'nodes_1'=8,'nodes_2'=4,'params'=2] {'params'}, dimensions={0} | all-to-all | bytes 1048576 | tf_op jit(solution)/shard_map/all_to_all | solution.py:16
  463.6 7.7 %all-to-all-start.25 = ((f32[32,1,4096]{2,1,0:T(1,128)}), f32[32,1,4096]{2,1,0:T(1,128)}, u32[]{:S(2)}, u32[]{:S(2)}) async-start(f32[32,1,4096]{2,1,0:T(1,128)} %reshape.126), calls=%async_computation.25 | async-start | bytes 1048576 | tf_op jit(solution)/shard_map/all_to_all | solution.py:16
  473.8 10.3 %all-to-all-done.25 = f32[32,1,4096]{2,1,0:T(1,128)} async-done(((f32[32,1,4096]{2,1,0:T(1,128)}), f32[32,1,4096]{2,1,0:T(1,128)}, u32[]{:S(2)}, u32[]{:S(2)}) %all-to-all-start.25) | async-done | bytes 524320 | tf_op jit(solution)/shard_map/all_to_all | solution.py:16
  484.0 8.1 %all-to-all-start.27 = ((f32[32,1,4096]{2,1,0:T(1,128)}), f32[32,1,4096]{2,1,0:T(1,128)}, u32[]{:S(2)}, u32[]{:S(2)}) async-start(f32[32,1,4096]{2,1,0:T(1,128)} %reshape.122), calls=%async_computation.27 | async-start | bytes 1048576 | tf_op jit(solution)/shard_map/all_to_all | solution.py:16
  519.0 6.3 %all_to_all.166 = f32[2,1,4096]{2,1,0:T(1,128)S(1)} all-to-all(f32[2,1,4096]{2,1,0:T(1,128)S(1)} %reshape.132), channel_id=1, replica_groups=mesh['nodes_0'=4,'nodes_1'=8,'nodes_2'=4,'params'=2] {'params'}, dimensions={0} | all-to-all | bytes 65536 | tf_op jit(solution)/shard_map/all_to_all | solution.py:16
  538.0 9.9 %all-to-all-start.30 = ((f32[32,1,3072]{2,1,0:T(1,128)}), f32[32,1,3072]{2,1,0:T(1,128)S(1)}, u32[]{:S(2)}, u32[]{:S(2)}) async-start(f32[32,1,3072]{2,1,0:T(1,128)} %reshape.130), calls=%async_computation.30 | async-start | bytes 786432 | tf_op jit(solution)/shard_map/all_to_all | solution.py:16
  564.1 5.8 cholesky.315
  580.2 7.0 %all_to_all.167 = f32[2,64,1024]{2,1,0:T(8,128)S(1)} all-to-all(f32[2,64,1024]{2,1,0:T(8,128)S(1)} %broadcast_in_dim.152), channel_id=1, replica_groups=mesh['nodes_0'=4,'nodes_1'=8,'nodes_2'=4,'params'=2] {'params'}, dimensions={0} | all-to-all | bytes 1048576 | tf_op jit(solution)/shard_map/all_to_all | solution.py:16
  (358 shorter events, 332.3 us)
Async XLA Ops:
  2.8 10.4 %all-to-all-start = ((f32[4,1,4096]{2,1,0:T(1,128)}), f32[4,1,4096]{2,1,0:T(1,128)S(1)}, u32[]{:S(2)}, u32[]{:S(2)}) async-start(f32[4,1,4096]{2,1,0:T(1,128)} %reshape.82), calls=%async_computation | async-start | bytes 131072 | tf_op jit(solution)/shard_map/all_to_all | solution.py:16
  13.2 8.7 %all-to-all-start.2 = ((f32[4,1,4096]{2,1,0:T(1,128)}), f32[4,1,4096]{2,1,0:T(1,128)S(1)}, u32[]{:S(2)}, u32[]{:S(2)}) async-start(f32[4,1,4096]{2,1,0:T(1,128)} %reshape.78), calls=%async_computation.2 | async-start | bytes 131072 | tf_op jit(solution)/shard_map/all_to_all | solution.py:16
  21.9 23.5 %all-to-all-start.1 = ((f32[32,1,4096]{2,1,0:T(1,128)}), f32[32,1,4096]{2,1,0:T(1,128)S(1)}, u32[]{:S(2)}, u32[]{:S(2)}) async-start(f32[32,1,4096]{2,1,0:T(1,128)} %reshape.84), calls=%async_computation.1 | async-start | bytes 1048576 | tf_op jit(solution)/shard_map/all_to_all | solution.py:16
  45.4 0.8 copy-start
  46.3 25.1 %all-to-all-start.3 = ((f32[32,1,4096]{2,1,0:T(1,128)}), f32[32,1,4096]{2,1,0:T(1,128)}, u32[]{:S(2)}, u32[]{:S(2)}) async-start(f32[32,1,4096]{2,1,0:T(1,128)} %reshape.80), calls=%async_computation.3 | async-start | bytes 1048576 | tf_op jit(solution)/shard_map/all_to_all | solution.py:16
  54.1 3.6 copy-start.3
  84.6 8.6 %all-to-all-start.5 = ((f32[8,1,3072]{2,1,0:T(1,128)}), f32[8,1,3072]{2,1,0:T(1,128)S(1)}, u32[]{:S(2)}, u32[]{:S(2)}) async-start(f32[8,1,3072]{2,1,0:T(1,128)} %reshape.86), calls=%async_computation.5 | async-start | bytes 196608 | tf_op jit(solution)/shard_map/all_to_all | solution.py:16
  95.5 21.7 %all-to-all-start.6 = ((f32[32,1,3072]{2,1,0:T(1,128)}), f32[32,1,3072]{2,1,0:T(1,128)S(1)}, u32[]{:S(2)}, u32[]{:S(2)}) async-start(f32[32,1,3072]{2,1,0:T(1,128)} %reshape.88), calls=%async_computation.6 | async-start | bytes 786432 | tf_op jit(solution)/shard_map/all_to_all | solution.py:16
  146.3 13.5 %all-to-all-start.8 = ((f32[4,1,4096]{2,1,0:T(1,128)}), f32[4,1,4096]{2,1,0:T(1,128)S(1)}, u32[]{:S(2)}, u32[]{:S(2)}) async-start(f32[4,1,4096]{2,1,0:T(1,128)} %reshape.96), calls=%async_computation.8 | async-start | bytes 131072 | tf_op jit(solution)/shard_map/all_to_all | solution.py:16
  159.8 8.7 %all-to-all-start.10 = ((f32[4,1,4096]{2,1,0:T(1,128)}), f32[4,1,4096]{2,1,0:T(1,128)S(1)}, u32[]{:S(2)}, u32[]{:S(2)}) async-start(f32[4,1,4096]{2,1,0:T(1,128)} %reshape.92), calls=%async_computation.10 | async-start | bytes 131072 | tf_op jit(solution)/shard_map/all_to_all | solution.py:16
  168.5 20.2 %all-to-all-start.9 = ((f32[32,1,4096]{2,1,0:T(1,128)}), f32[32,1,4096]{2,1,0:T(1,128)}, u32[]{:S(2)}, u32[]{:S(2)}) async-start(f32[32,1,4096]{2,1,0:T(1,128)} %reshape.98), calls=%async_computation.9 | async-start | bytes 1048576 | tf_op jit(solution)/shard_map/all_to_all | solution.py:16
  188.7 26.9 %all-to-all-start.11 = ((f32[32,1,4096]{2,1,0:T(1,128)}), f32[32,1,4096]{2,1,0:T(1,128)}, u32[]{:S(2)}, u32[]{:S(2)}) async-start(f32[32,1,4096]{2,1,0:T(1,128)} %reshape.94), calls=%async_computation.11 | async-start | bytes 1048576 | tf_op jit(solution)/shard_map/all_to_all | solution.py:16
  231.7 8.6 %all-to-all-start.13 = ((f32[8,1,3072]{2,1,0:T(1,128)}), f32[8,1,3072]{2,1,0:T(1,128)S(1)}, u32[]{:S(2)}, u32[]{:S(2)}) async-start(f32[8,1,3072]{2,1,0:T(1,128)} %reshape.100), calls=%async_computation.13 | async-start | bytes 196608 | tf_op jit(solution)/shard_map/all_to_all | solution.py:16
  242.6 22.1 %all-to-all-start.14 = ((f32[32,1,3072]{2,1,0:T(1,128)}), f32[32,1,3072]{2,1,0:T(1,128)S(1)}, u32[]{:S(2)}, u32[]{:S(2)}) async-start(f32[32,1,3072]{2,1,0:T(1,128)} %reshape.102), calls=%async_computation.14 | async-start | bytes 786432 | tf_op jit(solution)/shard_map/all_to_all | solution.py:16
  298.5 8.6 %all-to-all-start.16 = ((f32[4,1,4096]{2,1,0:T(1,128)}), f32[4,1,4096]{2,1,0:T(1,128)S(1)}, u32[]{:S(2)}, u32[]{:S(2)}) async-start(f32[4,1,4096]{2,1,0:T(1,128)} %reshape.110), calls=%async_computation.16 | async-start | bytes 131072 | tf_op jit(solution)/shard_map/all_to_all | solution.py:16
  307.1 8.7 %all-to-all-start.18 = ((f32[4,1,4096]{2,1,0:T(1,128)}), f32[4,1,4096]{2,1,0:T(1,128)S(1)}, u32[]{:S(2)}, u32[]{:S(2)}) async-start(f32[4,1,4096]{2,1,0:T(1,128)} %reshape.106), calls=%async_computation.18 | async-start | bytes 131072 | tf_op jit(solution)/shard_map/all_to_all | solution.py:16
  315.8 20.5 %all-to-all-start.17 = ((f32[32,1,4096]{2,1,0:T(1,128)}), f32[32,1,4096]{2,1,0:T(1,128)}, u32[]{:S(2)}, u32[]{:S(2)}) async-start(f32[32,1,4096]{2,1,0:T(1,128)} %reshape.112), calls=%async_computation.17 | async-start | bytes 1048576 | tf_op jit(solution)/shard_map/all_to_all | solution.py:16
  336.3 27.1 %all-to-all-start.19 = ((f32[32,1,4096]{2,1,0:T(1,128)}), f32[32,1,4096]{2,1,0:T(1,128)}, u32[]{:S(2)}, u32[]{:S(2)}) async-start(f32[32,1,4096]{2,1,0:T(1,128)} %reshape.108), calls=%async_computation.19 | async-start | bytes 1048576 | tf_op jit(solution)/shard_map/all_to_all | solution.py:16
  379.5 8.6 %all-to-all-start.21 = ((f32[8,1,3072]{2,1,0:T(1,128)}), f32[8,1,3072]{2,1,0:T(1,128)S(1)}, u32[]{:S(2)}, u32[]{:S(2)}) async-start(f32[8,1,3072]{2,1,0:T(1,128)} %reshape.114), calls=%async_computation.21 | async-start | bytes 196608 | tf_op jit(solution)/shard_map/all_to_all | solution.py:16
  390.4 22.1 %all-to-all-start.22 = ((f32[32,1,3072]{2,1,0:T(1,128)}), f32[32,1,3072]{2,1,0:T(1,128)S(1)}, u32[]{:S(2)}, u32[]{:S(2)}) async-start(f32[32,1,3072]{2,1,0:T(1,128)} %reshape.116), calls=%async_computation.22 | async-start | bytes 786432 | tf_op jit(solution)/shard_map/all_to_all | solution.py:16
  446.4 8.5 %all-to-all-start.24 = ((f32[4,1,4096]{2,1,0:T(1,128)}), f32[4,1,4096]{2,1,0:T(1,128)S(1)}, u32[]{:S(2)}, u32[]{:S(2)}) async-start(f32[4,1,4096]{2,1,0:T(1,128)} %reshape.124), calls=%async_computation.24 | async-start | bytes 131072 | tf_op jit(solution)/shard_map/all_to_all | solution.py:16
  454.9 8.7 %all-to-all-start.26 = ((f32[4,1,4096]{2,1,0:T(1,128)}), f32[4,1,4096]{2,1,0:T(1,128)S(1)}, u32[]{:S(2)}, u32[]{:S(2)}) async-start(f32[4,1,4096]{2,1,0:T(1,128)} %reshape.120), calls=%async_computation.26 | async-start | bytes 131072 | tf_op jit(solution)/shard_map/all_to_all | solution.py:16
  463.6 20.5 %all-to-all-start.25 = ((f32[32,1,4096]{2,1,0:T(1,128)}), f32[32,1,4096]{2,1,0:T(1,128)}, u32[]{:S(2)}, u32[]{:S(2)}) async-start(f32[32,1,4096]{2,1,0:T(1,128)} %reshape.126), calls=%async_computation.25 | async-start | bytes 1048576 | tf_op jit(solution)/shard_map/all_to_all | solution.py:16
  484.0 26.9 %all-to-all-start.27 = ((f32[32,1,4096]{2,1,0:T(1,128)}), f32[32,1,4096]{2,1,0:T(1,128)}, u32[]{:S(2)}, u32[]{:S(2)}) async-start(f32[32,1,4096]{2,1,0:T(1,128)} %reshape.122), calls=%async_computation.27 | async-start | bytes 1048576 | tf_op jit(solution)/shard_map/all_to_all | solution.py:16
  516.7 31.2 %copy-start.1 = (f32[64,64]{1,0:T(8,128)}, f32[64,64]{1,0:T(8,128)S(1)}, u32[]{:S(2)}) copy-start(f32[64,64]{1,0:T(8,128)S(1)} %fusion.36) | copy-start | bytes 49156
  527.1 8.6 %all-to-all-start.29 = ((f32[8,1,3072]{2,1,0:T(1,128)}), f32[8,1,3072]{2,1,0:T(1,128)S(1)}, u32[]{:S(2)}, u32[]{:S(2)}) async-start(f32[8,1,3072]{2,1,0:T(1,128)} %reshape.128), calls=%async_computation.29 | async-start | bytes 196608 | tf_op jit(solution)/shard_map/all_to_all | solution.py:16
  538.0 22.2 %all-to-all-start.30 = ((f32[32,1,3072]{2,1,0:T(1,128)}), f32[32,1,3072]{2,1,0:T(1,128)S(1)}, u32[]{:S(2)}, u32[]{:S(2)}) async-start(f32[32,1,3072]{2,1,0:T(1,128)} %reshape.130), calls=%async_computation.30 | async-start | bytes 786432 | tf_op jit(solution)/shard_map/all_to_all | solution.py:16
  562.4 17.7 %copy-start.2 = (f32[64,48]{0,1:T(8,128)}, f32[64,48]{0,1:T(8,128)S(1)}, u32[]{:S(2)}) copy-start(f32[64,48]{0,1:T(8,128)S(1)} %fusion.31) | copy-start | bytes 36868
where the time goes:
time: 601 us; the launch traced here: 589 us
  other arithmetic  199 us (33%)
  starting transfers between devices  152 us (25%)
  matrix products  65.2 us (11%)
  waiting for transfers between devices  62.8 us (10%)
  blocking collectives  54 us (9%)
  local copies, waits for them, and re-layouts  46.1 us (8%)
  between operations  10.5 us (2%)
    all_to_all x24, starting transfers between devices, copy_for_each(): return lax.all_to_all(copies, axis, split_axis=0, concat_axis=0, tiled=True)  152 us
    another operation x36, other arithmetic, solve_gram(): chol_factor = jnp.linalg.cholesky(matrix)  78.2 us
    another operation x24, other arithmetic, solve_gram(): return jax.scipy.linalg.cho_solve((chol_factor, True), right_side)  66.6 us
    all_to_all x24, waiting for transfers between devices, copy_for_each(): return lax.all_to_all(copies, axis, split_axis=0, concat_axis=0, tiled=True)  62.8 us
    all_to_all x8, blocking collectives, copy_for_each(): return lax.all_to_all(copies, axis, split_axis=0, concat_axis=0, tiled=True)  54 us
    all_to_all x28, other arithmetic, copy_for_each(): return lax.all_to_all(copies, axis, split_axis=0, concat_axis=0, tiled=True)  47.6 us
    unnamed x73, local copies, waits for them, and re-layouts  39.5 us
    dot_general x4, matrix products, per_device(): jnp.dot(unfolded, space_low.T, preferred_element_type=jnp.float32)  19.1 us
  transfers between devices with their start and end apart: 24, of which 12 were waited for; matrix products, arithmetic and copies ran while one was open for 29% of the time, Pallas kernels for 0%

commit v1 on v0

v1 whole, which is shorter than its diff:
```python
import functools

import jax
import jax.numpy as jnp
from jax import lax
from jax.experimental import pallas as pl
from jax.experimental.pallas import tpu as pltpu
from jax.sharding import Mesh
from jax.sharding import PartitionSpec as P

SWEEPS = 4
NODES = ("nodes_0", "nodes_1", "nodes_2")
PLANE = ("nodes_0", "nodes_2")
LINE = "nodes_1"
CORE = "params"
F32 = jnp.float32
BF16 = jnp.bfloat16
EXACT = lax.Precision.HIGHEST
RIDGE_SHARE = 0.01


def dot(a, b, over, precision=None):
    return lax.dot_general(
        a, b, (((over[0],), (over[1],)), ((), ())), precision=precision, preferred_element_type=F32
    )


def gram_rows(a):
    return dot(a, a, (0, 0), EXACT)


def row_of(x, i):
    return jnp.broadcast_to(x[i : i + 1, :], (8, x.shape[1]))


def column_of(x, i):
    return jnp.broadcast_to(x[:, i : i + 1], x.shape)


def eliminate(blocks):
    blocks = list(blocks)
    count = len(blocks)
    sub = lax.broadcasted_iota(jnp.int32, blocks[0].shape, 0)
    for k in range(count):
        lead = [column_of(blocks[k], 8 * k + i) for i in range(8)]
        others = {m: [column_of(blocks[m], 8 * k + i) for i in range(8)] for m in range(count) if m != k}
        rows = blocks[k]
        for i in range(8):
            pivot = sub == i
            factor = jnp.where(pivot, -1.0, lead[i]) * (1.0 / row_of(lead[i], i))
            rows = jnp.where(pivot, 0.0, rows) - factor * row_of(rows, i)
            for n in range(i + 1, 8):
                lead[n] = jnp.where(pivot, 0.0, lead[n]) - factor * row_of(lead[n], i)
        pivots = [row_of(rows, i) for i in range(8)]
        blocks[k] = rows
        for m, columns in others.items():
            terms = [columns[i] * pivots[i] for i in range(8)]
            while len(terms) > 1:
                terms = [terms[i] + terms[i + 1] for i in range(0, len(terms), 2)]
            blocks[m] = blocks[m] - terms[0]
    return blocks


def ridge_inverse(gram):
    n = gram.shape[0]
    row = lax.broadcasted_iota(jnp.int32, (n, n), 0)
    column = lax.broadcasted_iota(jnp.int32, (n, n), 1)
    eye = jnp.where(row == column, 1.0, 0.0).astype(F32)
    matrix = gram + (RIDGE_SHARE / n) * jnp.sum(gram * eye) * eye
    both = jnp.concatenate([matrix, eye], axis=1)
    done = eliminate([both[8 * m : 8 * m + 8, :] for m in range(n // 8)])
    return jnp.concatenate(done, axis=0)[:, n:]


def fold(x):
    half = x.shape[0] // 2
    return jnp.concatenate([x[:half, :], x[half:, :]], axis=1)


def unfold(x):
    half = x.shape[1] // 2
    return jnp.concatenate([x[:, :half], x[:, half:]], axis=0)


def total(parts):
    whole = [parts[i] for i in range(parts.shape[0])]
    while len(whole) > 1:
        whole = [whole[i] + whole[i + 1] for i in range(0, len(whole), 2)]
    return whole[0]


def contract(rows_ref, space, times_ref, contracted_ref, message_ref):
    rank = space.shape[0]
    steps = times_ref.shape[0]
    samples = message_ref.shape[0]
    low = space.astype(BF16)
    message_ref[:, rank:] = dot(space, space, (1, 1), EXACT)
    times = times_ref[...]
    group = 8
    for first in range(0, samples, group):
        part = dot(rows_ref[first * steps : (first + group) * steps, :], low, (1, 1))
        contracted_ref[first * steps : (first + group) * steps, :] = part
        sides = [
            jnp.sum(part[j * steps : (j + 1) * steps, :] * times, axis=0, keepdims=True) for j in range(group)
        ]
        message_ref[first : first + group, :rank] = jnp.concatenate(sides, axis=0)


def start_kernel(rows_ref, space_ref, times_ref, contracted_ref, message_ref):
    contract(rows_ref, space_ref[...], times_ref, contracted_ref, message_ref)


def space_kernel(rows_ref, own_ref, other_ref, inverse_ref, times_ref, space_ref, contracted_ref, message_ref):
    space = dot(inverse_ref[...], own_ref[...] + other_ref[...], (1, 0), EXACT)
    space_ref[...] = space
    contract(rows_ref, space, times_ref, contracted_ref, message_ref)


def last_kernel(own_ref, other_ref, inverse_ref, space_ref):
    space_ref[...] = dot(inverse_ref[...], own_ref[...] + other_ref[...], (1, 0), EXACT)


def params_kernel(parts_ref, times_ref, contracted_ref, params_ref, message_ref, space_gram_ref):
    steps, rank = times_ref.shape
    samples = params_ref.shape[0]
    whole = total(parts_ref)
    side, space_gram = whole[:, :rank], whole[:, rank:]
    space_gram_ref[...] = space_gram
    inverse = ridge_inverse(space_gram * gram_rows(times_ref[...]))
    params = dot(side, inverse, (1, 0), EXACT)
    params_ref[...] = params
    sums = [jnp.zeros((8, rank), F32) for _ in range(steps // 8)]
    for j in range(samples):
        factor = jnp.broadcast_to(params_ref[j : j + 1, :], (8, rank))
        for q in range(steps // 8):
            sums[q] = sums[q] + contracted_ref[j * steps + 8 * q : j * steps + 8 * q + 8, :] * factor
    message_ref[: steps // 2, :] = fold(jnp.concatenate(sums, axis=0))
    message_ref[steps // 2 :, :] = fold(gram_rows(params))


def inverse_kernel(first_ref, second_ref, inverse_ref):
    inverse_ref[...] = ridge_inverse(unfold(first_ref[...]) * second_ref[...])


def times_kernel(rows_ref, parts_ref, inverse_ref, params_ref, times_ref, gram_ref, side_ref, khatri_ref):
    steps, rank = times_ref.shape
    samples = params_ref.shape[0]
    times = dot(unfold(total(parts_ref)), inverse_ref[...], (1, 0), EXACT)
    times_ref[...] = times
    gram_ref[...] = gram_rows(times)
    for j in range(samples):
        factor = jnp.broadcast_to(params_ref[j : j + 1, :], times.shape)
        khatri_ref[j * steps : (j + 1) * steps, :] = (times * factor).astype(BF16)
    side_ref[...] = dot(khatri_ref[...], rows_ref[...], (0, 0))


def on_device(kernel, shapes, inputs, scratch=()):
    whole = pl.BlockSpec(memory_space=pltpu.VMEM)
    return pl.pallas_call(
        kernel,
        out_shape=[jax.ShapeDtypeStruct(shape, F32) for shape in shapes],
        in_specs=[whole] * inputs,
        out_specs=[whole] * len(shapes),
        scratch_shapes=list(scratch),
        compiler_params=pltpu.CompilerParams(vmem_limit_bytes=24 << 20),
    )


def copies(x, axes):
    everywhere = jnp.broadcast_to(x, (lax.axis_size(axes), *x.shape))
    return lax.all_to_all(everywhere, axes, split_axis=0, concat_axis=0, tiled=True)


def parts_of_nodes(x):
    return copies(jnp.sum(copies(x, PLANE), axis=0), LINE)


def other_core(x):
    return lax.ppermute(x, CORE, [(0, 1), (1, 0)])


def per_device(snapshots, space_start, time_start):
    samples, steps, nodes = snapshots.shape
    rank = space_start.shape[0]
    rows = snapshots.reshape(samples * steps, nodes)
    times = time_start.T
    start = on_device(start_kernel, [(samples * steps, rank), (samples, 2 * rank)], 3)
    again = on_device(space_kernel, [(rank, nodes), (samples * steps, rank), (samples, 2 * rank)], 5)
    last = on_device(last_kernel, [(rank, nodes)], 3)
    for_params = on_device(params_kernel, [(samples, rank), ((steps + rank) // 2, 2 * rank), (rank, rank)], 3)
    invert = on_device(inverse_kernel, [(rank, rank)], 2)
    for_times = on_device(
        times_kernel,
        [(steps, rank), (rank, rank), (rank, nodes)],
        4,
        [pltpu.VMEM((samples * steps, rank), BF16)],
    )
    contracted, message = start(rows, space_start, times)
    for sweep in range(SWEEPS):
        params, message, space_gram = for_params(parts_of_nodes(message), times, contracted)
        message = message + other_core(message)
        parts = parts_of_nodes(message[: steps // 2])
        param_gram = message[steps // 2 :]
        (inverse,) = invert(param_gram, space_gram)
        times, time_gram, side = for_times(rows, parts, inverse, params)
        (inverse,) = invert(param_gram, time_gram)
        other = other_core(side)
        if sweep + 1 < SWEEPS:
            space, contracted, message = again(rows, side, other, inverse, times)
        else:
            (space,) = last(side, other, inverse)
    return space, params.T, times.T


def solution(mesh):
    split = Mesh(
        mesh.devices.reshape(4, 8, 4, mesh.shape["params"]),
        ("nodes_0", "nodes_1", "nodes_2", "params"),
    )
    return jax.shard_map(
        per_device,
        mesh=split,
        in_specs=(P("params", None, NODES), P(None, NODES), P()),
        out_specs=(P(None, NODES), P(None, "params"), P()),
        check_vma=False,
    )
```

time: 601 us -> 292 us (0.49); the launches traced: 589 us -> 290 us
  other arithmetic: 199 us -> 0.24 us
  starting transfers between devices: 152 us -> 37 us
  blocking collectives: 54 us -> 156 us
  matrix products: 65.2 us -> 0 us
  Pallas kernels: 0 us -> 46.2 us
  waiting for transfers between devices: 62.8 us -> 25.5 us
  local copies, waits for them, and re-layouts: 46.1 us -> 24.8 us
  between operations: 10.5 us -> 0.93 us
    another operation x60 -> x0, other arithmetic: 145 us -> none  [the longest x36 78.2 us: solve_gram(): chol_factor = jnp.linalg.cholesky(matrix)]
    all_to_all x24 -> x4, starting transfers between devices: 152 us -> 13.7 us  [copies(): lax.all_to_all(everywhere, axes, split_axis=0, concat_axis=0, tiled=True)]
    all_to_all x8 -> x12, blocking collectives: 54 us -> 156 us  [copies(): lax.all_to_all(everywhere, axes, split_axis=0, concat_axis=0, tiled=True)]
    dot_general x27 -> x0, matrix products: 58.5 us -> none  [the longest x4 19.1 us: per_device(): jnp.dot(unfolded, space_low.T, preferred_element_type=jnp.float32)]
    all_to_all x28 -> x0, other arithmetic: 47.6 us -> none  [copy_for_each(): return lax.all_to_all(copies, axis, split_axis=0, concat_axis=0, tiled=True)]
    pallas_call x0 -> x21, Pallas kernels: none -> 46.2 us  [the longest x4 14.6 us: per_device(): for_params(parts_of_nodes(message), times, contracted)]
    all_to_all x24 -> x4, waiting for transfers between devices: 62.8 us -> 22.1 us  [copies(): lax.all_to_all(everywhere, axes, split_axis=0, concat_axis=0, tiled=True)]
    ppermute x0 -> x8, starting transfers between devices: none -> 23.4 us  [other_core(): return lax.ppermute(x, CORE, [(0, 1), (1, 0)])]
  transfers between devices with their start and end apart: 24 -> 12, of which waited for: 12 -> 8; matrix products, arithmetic and copies ran while one was open for 29% -> 0% of each run, Pallas kernels for 0% -> 5%
where the time goes in v1:
time: 292 us; the launch traced here: 290 us
  blocking collectives  156 us (53%)
  Pallas kernels  46.2 us (16%)
  starting transfers between devices  37 us (13%)
  waiting for transfers between devices  25.5 us (9%)
  local copies, waits for them, and re-layouts  24.8 us (8%)
    all_to_all x12, blocking collectives, copies(): lax.all_to_all(everywhere, axes, split_axis=0, concat_axis=0, tiled=True)  156 us
    ppermute x8, starting transfers between devices, other_core(): return lax.ppermute(x, CORE, [(0, 1), (1, 0)])  23.4 us
    all_to_all x4, waiting for transfers between devices, copies(): lax.all_to_all(everywhere, axes, split_axis=0, concat_axis=0, tiled=True)  22.1 us
    unnamed x23, local copies, waits for them, and re-layouts  21.9 us
    pallas_call x4, Pallas kernels, per_device(): for_params(parts_of_nodes(message), times, contracted)  14.6 us
    all_to_all x4, starting transfers between devices, copies(): lax.all_to_all(everywhere, axes, split_axis=0, concat_axis=0, tiled=True)  13.7 us
    pallas_call x4, Pallas kernels, per_device(): inverse, = invert(param_gram, space_gram)  7.83 us
    pallas_call x4, Pallas kernels, per_device(): inverse, = invert(param_gram, time_gram)  7.83 us
  transfers between devices with their start and end apart: 12, of which 8 were waited for; matrix products, arithmetic and copies ran while one was open for 0% of the time, Pallas kernels for 5%

profile of v1, /device:TPU:1, one launch (start us, length us, event | category | flops | bytes accessed | tf_op | source)
XLA Modules:
  0.0 290.3 jit_solution(7129782988030828280)
XLA Ops:
  7.2 17.8 %all_to_all.80 = f32[16,64,128]{2,1,0:T(8,128)S(1)} all-to-all(f32[16,64,128]{2,1,0:T(8,128)S(1)} %broadcast_in_dim.48), channel_id=1, replica_groups=mesh['nodes_0'=4,'nodes_1'=8,'nodes_2'=4,'params'=2] {'nodes_0','nodes_2'}, dimensions={0} | all-to-all | bytes 1048576 | tf_op jit(solution)/shard_map/all_to_all | solution.py:171
  25.0 17.4 %all_to_all.81.parts_ref = f32[8,64,128]{2,1,0:T(8,128)S(1)} all-to-all(f32[8,64,128]{2,1,0:T(8,128)S(1)} %broadcast_in_dim.49), channel_id=1, replica_groups=mesh['nodes_0'=4,'nodes_1'=8,'nodes_2'=4,'params'=2] {'nodes_1'}, dimensions={0} | all-to-all | bytes 524288 | tf_op jit(solution)/shard_map/all_to_all | solution.py:171
  42.5 3.6 %shard_map.59 = (f32[64,64]{1,0:T(8,128)S(1)}, f32[56,128]{1,0:T(8,128)S(1)}, f32[64,64]{1,0:T(8,128)S(1)}) custom-call(f32[8,64,128]{2,1,0:T(8,128)S(1)} %all_to_all.81.parts_ref, f32[48,64]{1,0:T(8,128)S(1)} %bitcast.14, f32[3072,64]{1,0:T(8,128)S(1)} %get-tuple-element.36.contracted_ref), custom_call_target="tpu_custom_call" | custom-call | tf_op jit(solution)/shard_map/pallas_call | solution.py:200
  46.1 3.5 %collective-permute-start = (f32[56,128]{1,0:T(8,128)S(1)}, f32[56,128]{1,0:T(8,128)S(1)}, u32[]{:S(2)}, u32[]{:S(2)}) collective-permute-start(f32[56,128]{1,0:T(8,128)S(1)} %get-tuple-element.37), channel_id=1, source_target_pairs={{0,1},{1,0},{2,3},{3,2},{4,5},{5,4},{6,7},{7,6},{8,9},{9,8},{10,11... | collective-permute-start | bytes 86024 | tf_op jit(solution)/shard_map/ppermute | solution.py:179
  50.5 10.5 %all_to_all.82 = f32[16,24,128]{2,1,0:T(8,128)S(1)} all-to-all(f32[16,24,128]{2,1,0:T(8,128)S(1)} %broadcast_in_dim.50), channel_id=1, replica_groups=mesh['nodes_0'=4,'nodes_1'=8,'nodes_2'=4,'params'=2] {'nodes_0','nodes_2'}, dimensions={0} | all-to-all | bytes 393216 | tf_op jit(solution)/shard_map/all_to_all | solution.py:171
  61.6 3.4 %all-to-all-start.3 = ((f32[8,24,128]{2,1,0:T(8,128)}), f32[8,24,128]{2,1,0:T(8,128)S(1)}, u32[]{:S(2)}, u32[]{:S(2)}) async-start(f32[8,24,128]{2,1,0:T(8,128)} %broadcast_in_dim.51), calls=%async_computation.3 | async-start | bytes 196608 | tf_op jit(solution)/shard_map/all_to_all | solution.py:171
  66.9 5.6 %all-to-all-done.3.parts_ref = f32[8,24,128]{2,1,0:T(8,128)S(1)} async-done(((f32[8,24,128]{2,1,0:T(8,128)}), f32[8,24,128]{2,1,0:T(8,128)S(1)}, u32[]{:S(2)}, u32[]{:S(2)}) %all-to-all-start.3) | async-done | bytes 98336 | tf_op jit(solution)/shard_map/all_to_all | solution.py:171
  72.5 2.8 copy-done.1
  76.9 3.0 %collective-permute-start.1 = (f32[64,1024]{1,0:T(8,128)S(1)}, f32[64,1024]{1,0:T(8,128)S(1)}, u32[]{:S(2)}, u32[]{:S(2)}) collective-permute-start(f32[64,1024]{1,0:T(8,128)S(1)} %get-tuple-element.40.own_ref), channel_id=1, source_target_pairs={{0,1},{1,0},{2,3},{3,2},{4,5},{5,4},{6,7},{7,6},{8,9},{9,8},{10,11... | collective-permute-start | bytes 786440 | tf_op jit(solution)/shard_map/ppermute | solution.py:179
  84.1 13.8 %all_to_all.83 = f32[16,64,128]{2,1,0:T(8,128)S(1)} all-to-all(f32[16,64,128]{2,1,0:T(8,128)S(1)} %broadcast_in_dim.52), channel_id=1, replica_groups=mesh['nodes_0'=4,'nodes_1'=8,'nodes_2'=4,'params'=2] {'nodes_0','nodes_2'}, dimensions={0} | all-to-all | bytes 1048576 | tf_op jit(solution)/shard_map/all_to_all | solution.py:171
  97.9 12.7 %all_to_all.84.parts_ref = f32[8,64,128]{2,1,0:T(8,128)S(1)} all-to-all(f32[8,64,128]{2,1,0:T(8,128)S(1)} %broadcast_in_dim.53), channel_id=1, replica_groups=mesh['nodes_0'=4,'nodes_1'=8,'nodes_2'=4,'params'=2] {'nodes_1'}, dimensions={0} | all-to-all | bytes 524288 | tf_op jit(solution)/shard_map/all_to_all | solution.py:171
  110.6 3.6 %shard_map.64 = (f32[64,64]{1,0:T(8,128)S(1)}, f32[56,128]{1,0:T(8,128)S(1)}, f32[64,64]{1,0:T(8,128)S(1)}) custom-call(f32[8,64,128]{2,1,0:T(8,128)S(1)} %all_to_all.84.parts_ref, f32[48,64]{1,0:T(8,128)S(1)} %get-tuple-element.42.times_ref, f32[3072,64]{1,0:T(8,128)S(1)} %get-tuple-element.44.contracted_ref), custom_call_target="tpu_custom_call" | custom-call | tf_op jit(solution)/shard_map/pallas_call | solution.py:200
  117.8 10.3 %all_to_all.85 = f32[16,24,128]{2,1,0:T(8,128)S(1)} all-to-all(f32[16,24,128]{2,1,0:T(8,128)S(1)} %broadcast_in_dim.54), channel_id=1, replica_groups=mesh['nodes_0'=4,'nodes_1'=8,'nodes_2'=4,'params'=2] {'nodes_0','nodes_2'}, dimensions={0} | all-to-all | bytes 393216 | tf_op jit(solution)/shard_map/all_to_all | solution.py:171
  128.7 3.4 %all-to-all-start.7 = ((f32[8,24,128]{2,1,0:T(8,128)}), f32[8,24,128]{2,1,0:T(8,128)S(1)}, u32[]{:S(2)}, u32[]{:S(2)}) async-start(f32[8,24,128]{2,1,0:T(8,128)} %broadcast_in_dim.55), calls=%async_computation.7 | async-start | bytes 196608 | tf_op jit(solution)/shard_map/all_to_all | solution.py:171
  134.0 5.6 %all-to-all-done.7.parts_ref = f32[8,24,128]{2,1,0:T(8,128)S(1)} async-done(((f32[8,24,128]{2,1,0:T(8,128)}), f32[8,24,128]{2,1,0:T(8,128)S(1)}, u32[]{:S(2)}, u32[]{:S(2)}) %all-to-all-start.7) | async-done | bytes 98336 | tf_op jit(solution)/shard_map/all_to_all | solution.py:171
  139.6 2.8 copy-done.3
  144.0 3.0 %collective-permute-start.3 = (f32[64,1024]{1,0:T(8,128)S(1)}, f32[64,1024]{1,0:T(8,128)S(1)}, u32[]{:S(2)}, u32[]{:S(2)}) collective-permute-start(f32[64,1024]{1,0:T(8,128)S(1)} %get-tuple-element.48.own_ref), channel_id=1, source_target_pairs={{0,1},{1,0},{2,3},{3,2},{4,5},{5,4},{6,7},{7,6},{8,9},{9,8},{10,11... | collective-permute-start | bytes 786440 | tf_op jit(solution)/shard_map/ppermute | solution.py:179
  148.9 2.8 copy-done.4
  153.9 13.7 %all_to_all.86 = f32[16,64,128]{2,1,0:T(8,128)S(1)} all-to-all(f32[16,64,128]{2,1,0:T(8,128)S(1)} %broadcast_in_dim.56), channel_id=1, replica_groups=mesh['nodes_0'=4,'nodes_1'=8,'nodes_2'=4,'params'=2] {'nodes_0','nodes_2'}, dimensions={0} | all-to-all | bytes 1048576 | tf_op jit(solution)/shard_map/all_to_all | solution.py:171
  167.8 12.6 %all_to_all.87.parts_ref = f32[8,64,128]{2,1,0:T(8,128)S(1)} all-to-all(f32[8,64,128]{2,1,0:T(8,128)S(1)} %broadcast_in_dim.57), channel_id=1, replica_groups=mesh['nodes_0'=4,'nodes_1'=8,'nodes_2'=4,'params'=2] {'nodes_1'}, dimensions={0} | all-to-all | bytes 524288 | tf_op jit(solution)/shard_map/all_to_all | solution.py:171
  180.4 3.6 %shard_map.69 = (f32[64,64]{1,0:T(8,128)S(1)}, f32[56,128]{1,0:T(8,128)S(1)}, f32[64,64]{1,0:T(8,128)S(1)}) custom-call(f32[8,64,128]{2,1,0:T(8,128)S(1)} %all_to_all.87.parts_ref, f32[48,64]{1,0:T(8,128)S(1)} %get-tuple-element.50.times_ref, f32[3072,64]{1,0:T(8,128)S(1)} %get-tuple-element.52.contracted_ref), custom_call_target="tpu_custom_call" | custom-call | tf_op jit(solution)/shard_map/pallas_call | solution.py:200
  187.6 10.3 %all_to_all.88 = f32[16,24,128]{2,1,0:T(8,128)S(1)} all-to-all(f32[16,24,128]{2,1,0:T(8,128)S(1)} %broadcast_in_dim.58), channel_id=1, replica_groups=mesh['nodes_0'=4,'nodes_1'=8,'nodes_2'=4,'params'=2] {'nodes_0','nodes_2'}, dimensions={0} | all-to-all | bytes 393216 | tf_op jit(solution)/shard_map/all_to_all | solution.py:171
  198.5 3.6 %all-to-all-start.11 = ((f32[8,24,128]{2,1,0:T(8,128)}), f32[8,24,128]{2,1,0:T(8,128)S(1)}, u32[]{:S(2)}, u32[]{:S(2)}) async-start(f32[8,24,128]{2,1,0:T(8,128)} %broadcast_in_dim.59), calls=%async_computation.11 | async-start | bytes 196608 | tf_op jit(solution)/shard_map/all_to_all | solution.py:171
  204.1 5.3 %all-to-all-done.11.parts_ref = f32[8,24,128]{2,1,0:T(8,128)S(1)} async-done(((f32[8,24,128]{2,1,0:T(8,128)}), f32[8,24,128]{2,1,0:T(8,128)S(1)}, u32[]{:S(2)}, u32[]{:S(2)}) %all-to-all-start.11) | async-done | bytes 98336 | tf_op jit(solution)/shard_map/all_to_all | solution.py:171
  213.7 3.0 %collective-permute-start.5 = (f32[64,1024]{1,0:T(8,128)S(1)}, f32[64,1024]{1,0:T(8,128)S(1)}, u32[]{:S(2)}, u32[]{:S(2)}) collective-permute-start(f32[64,1024]{1,0:T(8,128)S(1)} %get-tuple-element.56.own_ref), channel_id=1, source_target_pairs={{0,1},{1,0},{2,3},{3,2},{4,5},{5,4},{6,7},{7,6},{8,9},{9,8},{10,11... | collective-permute-start | bytes 786440 | tf_op jit(solution)/shard_map/ppermute | solution.py:179
  223.8 13.7 %all_to_all.89 = f32[16,64,128]{2,1,0:T(8,128)S(1)} all-to-all(f32[16,64,128]{2,1,0:T(8,128)S(1)} %broadcast_in_dim.60), channel_id=1, replica_groups=mesh['nodes_0'=4,'nodes_1'=8,'nodes_2'=4,'params'=2] {'nodes_0','nodes_2'}, dimensions={0} | all-to-all | bytes 1048576 | tf_op jit(solution)/shard_map/all_to_all | solution.py:171
  237.6 12.6 %all_to_all.90.parts_ref = f32[8,64,128]{2,1,0:T(8,128)S(1)} all-to-all(f32[8,64,128]{2,1,0:T(8,128)S(1)} %broadcast_in_dim.61), channel_id=1, replica_groups=mesh['nodes_0'=4,'nodes_1'=8,'nodes_2'=4,'params'=2] {'nodes_1'}, dimensions={0} | all-to-all | bytes 524288 | tf_op jit(solution)/shard_map/all_to_all | solution.py:171
  250.2 3.6 %shard_map.74 = (f32[64,64]{1,0:T(8,128)S(1)}, f32[56,128]{1,0:T(8,128)S(1)}, f32[64,64]{1,0:T(8,128)S(1)}) custom-call(f32[8,64,128]{2,1,0:T(8,128)S(1)} %all_to_all.90.parts_ref, f32[48,64]{1,0:T(8,128)S(1)} %get-tuple-element.58.times_ref, f32[3072,64]{1,0:T(8,128)S(1)} %get-tuple-element.60.contracted_ref), custom_call_target="tpu_custom_call" | custom-call | tf_op jit(solution)/shard_map/pallas_call | solution.py:200
  257.5 10.3 %all_to_all.91 = f32[16,24,128]{2,1,0:T(8,128)S(1)} all-to-all(f32[16,24,128]{2,1,0:T(8,128)S(1)} %broadcast_in_dim.62), channel_id=1, replica_groups=mesh['nodes_0'=4,'nodes_1'=8,'nodes_2'=4,'params'=2] {'nodes_0','nodes_2'}, dimensions={0} | all-to-all | bytes 393216 | tf_op jit(solution)/shard_map/all_to_all | solution.py:171
  268.4 3.4 %all-to-all-start.15 = ((f32[8,24,128]{2,1,0:T(8,128)}), f32[8,24,128]{2,1,0:T(8,128)S(1)}, u32[]{:S(2)}, u32[]{:S(2)}) async-start(f32[8,24,128]{2,1,0:T(8,128)} %broadcast_in_dim.63), calls=%async_computation.15 | async-start | bytes 196608 | tf_op jit(solution)/shard_map/all_to_all | solution.py:171
  273.7 5.6 %all-to-all-done.15.parts_ref = f32[8,24,128]{2,1,0:T(8,128)S(1)} async-done(((f32[8,24,128]{2,1,0:T(8,128)}), f32[8,24,128]{2,1,0:T(8,128)S(1)}, u32[]{:S(2)}, u32[]{:S(2)}) %all-to-all-start.15) | async-done | bytes 98336 | tf_op jit(solution)/shard_map/all_to_all | solution.py:171
  283.6 3.0 %collective-permute-start.7 = (f32[64,1024]{1,0:T(8,128)S(1)}, f32[64,1024]{1,0:T(8,128)S(1)}, u32[]{:S(2)}, u32[]{:S(2)}) collective-permute-start(f32[64,1024]{1,0:T(8,128)S(1)} %get-tuple-element.64.own_ref), channel_id=1, source_target_pairs={{0,1},{1,0},{2,3},{3,2},{4,5},{5,4},{6,7},{7,6},{8,9},{9,8},{10,11... | collective-permute-start | bytes 786440 | tf_op jit(solution)/shard_map/ppermute | solution.py:179
  (84 shorter events, 59.7 us)
Async XLA Ops:
  0.6 2.8 copy-start
  3.4 0.9 copy-start.8
  4.4 0.7 copy-start.9
  7.1 35.4 %copy-start.10 = (f32[64,48]{0,1:T(8,128)S(1)}, f32[64,48]{0,1:T(8,128)}, u32[]{:S(2)}) copy-start(f32[64,48]{0,1:T(8,128)} %param.5) | copy-start | bytes 36868
  46.1 4.3 %collective-permute-start = (f32[56,128]{1,0:T(8,128)S(1)}, f32[56,128]{1,0:T(8,128)S(1)}, u32[]{:S(2)}, u32[]{:S(2)}) collective-permute-start(f32[56,128]{1,0:T(8,128)S(1)} %get-tuple-element.37), channel_id=1, source_target_pairs={{0,1},{1,0},{2,3},{3,2},{4,5},{5,4},{6,7},{7,6},{8,9},{9,8},{10,11... | collective-permute-start | bytes 86024 | tf_op jit(solution)/shard_map/ppermute | solution.py:179
  61.6 10.9 %all-to-all-start.3 = ((f32[8,24,128]{2,1,0:T(8,128)}), f32[8,24,128]{2,1,0:T(8,128)S(1)}, u32[]{:S(2)}, u32[]{:S(2)}) async-start(f32[8,24,128]{2,1,0:T(8,128)} %broadcast_in_dim.51), calls=%async_computation.3 | async-start | bytes 196608 | tf_op jit(solution)/shard_map/all_to_all | solution.py:171
  72.5 2.8 copy-start.1
  75.3 6.5 %copy-start.2 = (bf16[64,48,1024]{2,1,0:T(8,128)(2,1)S(1)}, bf16[64,48,1024]{2,1,0:T(8,128)(2,1)}, u32[]{:S(2)}) copy-start(bf16[64,48,1024]{2,1,0:T(8,128)(2,1)} %param.3) | copy-start | bytes 18874372
  76.9 4.9 %collective-permute-start.1 = (f32[64,1024]{1,0:T(8,128)S(1)}, f32[64,1024]{1,0:T(8,128)S(1)}, u32[]{:S(2)}, u32[]{:S(2)}) collective-permute-start(f32[64,1024]{1,0:T(8,128)S(1)} %get-tuple-element.40.own_ref), channel_id=1, source_target_pairs={{0,1},{1,0},{2,3},{3,2},{4,5},{5,4},{6,7},{7,6},{8,9},{9,8},{10,11... | collective-permute-start | bytes 786440 | tf_op jit(solution)/shard_map/ppermute | solution.py:179
  114.3 3.5 %collective-permute-start.2 = (f32[56,128]{1,0:T(8,128)S(1)}, f32[56,128]{1,0:T(8,128)S(1)}, u32[]{:S(2)}, u32[]{:S(2)}) collective-permute-start(f32[56,128]{1,0:T(8,128)S(1)} %get-tuple-element.45), channel_id=1, source_target_pairs={{0,1},{1,0},{2,3},{3,2},{4,5},{5,4},{6,7},{7,6},{8,9},{9,8},{10,11... | collective-permute-start | bytes 86024 | tf_op jit(solution)/shard_map/ppermute | solution.py:179
  128.7 10.9 %all-to-all-start.7 = ((f32[8,24,128]{2,1,0:T(8,128)}), f32[8,24,128]{2,1,0:T(8,128)S(1)}, u32[]{:S(2)}, u32[]{:S(2)}) async-start(f32[8,24,128]{2,1,0:T(8,128)} %broadcast_in_dim.55), calls=%async_computation.7 | async-start | bytes 196608 | tf_op jit(solution)/shard_map/all_to_all | solution.py:171
  139.6 2.8 copy-start.3
  144.0 4.9 %collective-permute-start.3 = (f32[64,1024]{1,0:T(8,128)S(1)}, f32[64,1024]{1,0:T(8,128)S(1)}, u32[]{:S(2)}, u32[]{:S(2)}) collective-permute-start(f32[64,1024]{1,0:T(8,128)S(1)} %get-tuple-element.48.own_ref), channel_id=1, source_target_pairs={{0,1},{1,0},{2,3},{3,2},{4,5},{5,4},{6,7},{7,6},{8,9},{9,8},{10,11... | collective-permute-start | bytes 786440 | tf_op jit(solution)/shard_map/ppermute | solution.py:179
  148.9 2.8 copy-start.4
  184.0 3.6 %collective-permute-start.4 = (f32[56,128]{1,0:T(8,128)S(1)}, f32[56,128]{1,0:T(8,128)S(1)}, u32[]{:S(2)}, u32[]{:S(2)}) collective-permute-start(f32[56,128]{1,0:T(8,128)S(1)} %get-tuple-element.53), channel_id=1, source_target_pairs={{0,1},{1,0},{2,3},{3,2},{4,5},{5,4},{6,7},{7,6},{8,9},{9,8},{10,11... | collective-permute-start | bytes 86024 | tf_op jit(solution)/shard_map/ppermute | solution.py:179
  198.5 10.9 %all-to-all-start.11 = ((f32[8,24,128]{2,1,0:T(8,128)}), f32[8,24,128]{2,1,0:T(8,128)S(1)}, u32[]{:S(2)}, u32[]{:S(2)}) async-start(f32[8,24,128]{2,1,0:T(8,128)} %broadcast_in_dim.59), calls=%async_computation.11 | async-start | bytes 196608 | tf_op jit(solution)/shard_map/all_to_all | solution.py:171
  209.4 2.8 copy-start.5
  213.7 5.0 %collective-permute-start.5 = (f32[64,1024]{1,0:T(8,128)S(1)}, f32[64,1024]{1,0:T(8,128)S(1)}, u32[]{:S(2)}, u32[]{:S(2)}) collective-permute-start(f32[64,1024]{1,0:T(8,128)S(1)} %get-tuple-element.56.own_ref), channel_id=1, source_target_pairs={{0,1},{1,0},{2,3},{3,2},{4,5},{5,4},{6,7},{7,6},{8,9},{9,8},{10,11... | collective-permute-start | bytes 786440 | tf_op jit(solution)/shard_map/ppermute | solution.py:179
  218.7 2.8 copy-start.6
  253.9 3.6 %collective-permute-start.6 = (f32[56,128]{1,0:T(8,128)S(1)}, f32[56,128]{1,0:T(8,128)S(1)}, u32[]{:S(2)}, u32[]{:S(2)}) collective-permute-start(f32[56,128]{1,0:T(8,128)S(1)} %get-tuple-element.61), channel_id=1, source_target_pairs={{0,1},{1,0},{2,3},{3,2},{4,5},{5,4},{6,7},{7,6},{8,9},{9,8},{10,11... | collective-permute-start | bytes 86024 | tf_op jit(solution)/shard_map/ppermute | solution.py:179
  268.4 10.9 %all-to-all-start.15 = ((f32[8,24,128]{2,1,0:T(8,128)}), f32[8,24,128]{2,1,0:T(8,128)S(1)}, u32[]{:S(2)}, u32[]{:S(2)}) async-start(f32[8,24,128]{2,1,0:T(8,128)} %broadcast_in_dim.63), calls=%async_computation.15 | async-start | bytes 196608 | tf_op jit(solution)/shard_map/all_to_all | solution.py:171
  279.3 2.8 copy-start.7
  283.6 5.6 %collective-permute-start.7 = (f32[64,1024]{1,0:T(8,128)S(1)}, f32[64,1024]{1,0:T(8,128)S(1)}, u32[]{:S(2)}, u32[]{:S(2)}) collective-permute-start(f32[64,1024]{1,0:T(8,128)S(1)} %get-tuple-element.64.own_ref), channel_id=1, source_target_pairs={{0,1},{1,0},{2,3},{3,2},{4,5},{5,4},{6,7},{7,6},{8,9},{9,8},{10,11... | collective-permute-start | bytes 786440 | tf_op jit(solution)/shard_map/ppermute | solution.py:179
